TPU v7x, 128 devices: a whole 4x4x4 slice. The times are simulated.
128 devices in a mesh: rows: 16 (over z, x), cols: 8 (over y, core).
Axes of the slice: x: 4, y: 4, z: 4, core: 2. Of those that a mesh axis runs over, the one named last changes fastest.
Arguments:
- points: float32 [160, 127], replicated, may hold values from -0.5 to 0.5
- noise: float32 [160, 128], replicated, may hold values from 0.3 to 3
- basis: float32 [20480, 128], P('rows'), may hold values from -0.5 to 0.5
Outputs:
- factor: float32 [20480, 20480], P('rows', 'cols')
All inputs are finite; a program needn't handle non-finite values.
Results may differ from a plain program's by a relative error of at most 0.0003.
Values sent between devices are 32-bit elements; how exact they have to be, the bound alone decides.
A program may use at most 128 MiB of HBM per device.

v0:
```python
import jax
import jax.numpy as jnp
from jax import lax
from jax.sharding import PartitionSpec as P

PW = 256
PANELS = 2
LEAD = 512


def from_root(x, axis, root):
    mine = lax.axis_index(axis) == root
    return lax.psum(jnp.where(mine, x, jnp.zeros_like(x)), axis)


def tile_rows(point_row, col_points):
    rho = point_row[None, :] - col_points
    kval = jnp.exp(-0.5 * jnp.sum(rho * rho, axis=1))
    ones = jnp.ones((col_points.shape[0], 1), jnp.float32)
    left = jnp.concatenate([ones, -rho], axis=1)
    right = jnp.concatenate([ones, rho], axis=1)
    width = left.shape[1]
    jmat = jnp.diag((jnp.arange(width) > 0).astype(jnp.float32))
    tiles = kval[None, :, None] * (jmat[:, None, :] + left.T[:, :, None] * right[None, :, :])
    return tiles.reshape(width, -1)


def point_rows(point_row, noise_row, basis_row, start, col_points, col_basis, col_start):
    width = noise_row.shape[0]
    values = tile_rows(point_row, col_points) + jnp.dot(
        basis_row, col_basis.T, precision=lax.Precision.HIGHEST
    )
    row_ids = start + jnp.arange(width)
    col_ids = col_start + jnp.arange(values.shape[1])
    same = row_ids[:, None] == col_ids[None, :]
    return values + jnp.where(same, noise_row[:, None], jnp.float32(0.0))


def assemble(points_rows, noise_rows, basis_rows, starts, col_points, col_basis, col_start):
    count, width = noise_rows.shape
    basis_split = basis_rows.reshape(count, width, -1)

    def assemble_single(items):
        return point_rows(items[0], items[1], items[2], items[3], col_points, col_basis, col_start)

    blocks = lax.map(assemble_single, (points_rows, noise_rows, basis_split, starts))
    return blocks.reshape(count * width, -1)


def mask_panel(panel, row_ids, low):
    col_ids = low + jnp.arange(panel.shape[1])
    return jnp.where(row_ids[:, None] < col_ids[None, :], jnp.float32(0.0), panel)


def finish(
    points_rows,
    noise_rows,
    basis_rows,
    starts,
    lead_rows,
    col_points,
    col_basis,
    col_start,
    lead_cols,
):
    count, width = noise_rows.shape
    ncols = lead_cols.shape[0]
    leading = lead_rows.shape[1]
    cross = lead_cols.T
    col_ids = col_start + jnp.arange(ncols)

    def finish_single(items):
        prow, nrow, brow, lrow, start = items
        values = point_rows(prow, nrow, brow, start, col_points, col_basis, col_start)
        trail = values - jnp.dot(lrow, cross, precision=lax.Precision.HIGHEST)
        row_ids = start + jnp.arange(width)
        own = jnp.pad(lrow, ((0, 0), (0, ncols - leading)))
        mirror = lax.dynamic_slice_in_dim(cross, jnp.minimum(start, leading - width), width, 0)
        inner = jnp.where(row_ids[:, None] < leading, mirror, trail)
        return jnp.where(col_ids[None, :] < leading, own, inner)

    blocks = lax.map(
        finish_single,
        (
            points_rows,
            noise_rows,
            basis_rows.reshape(count, width, -1),
            lead_rows.reshape(count, width, leading),
            starts,
        ),
    )
    return blocks.reshape(count * width, ncols)


def body(points, noise, basis):
    ratio = lax.axis_size("rows") // lax.axis_size("cols")
    row_pos = lax.axis_index("rows")
    col_pos = lax.axis_index("cols")
    width = noise.shape[1]
    rows_dev = basis.shape[0]
    row_pts = rows_dev // width
    col_pts = row_pts * ratio
    cols_dev = rows_dev * ratio
    row_start = row_pos * rows_dev
    col_start = col_pos * cols_dev
    row_points = lax.dynamic_slice_in_dim(points, row_pos * row_pts, row_pts, 0)
    row_noise = lax.dynamic_slice_in_dim(noise, row_pos * row_pts, row_pts, 0)
    col_points = lax.dynamic_slice_in_dim(points, col_pos * col_pts, col_pts, 0)
    pieces = []
    for step in range(ratio):
        pieces.append(from_root(basis, "rows", col_pos * ratio + step))
    col_basis = jnp.concatenate(pieces, axis=0)
    lead_points = LEAD // width
    row_starts = row_start + width * jnp.arange(row_pts)
    own_ids = row_start + jnp.arange(rows_dev)
    columns = assemble(
        row_points,
        row_noise,
        basis,
        row_starts,
        col_points[:lead_points],
        col_basis[:LEAD],
        col_start,
    )
    top_ids = jnp.arange(LEAD)
    lead_rows = None
    lead_top = None
    for panel_index in range(PANELS):
        low = panel_index * PW
        block = columns[:, low : low + PW]
        if lead_rows is not None:
            block = block - jnp.dot(
                lead_rows, lead_top[low : low + PW].T, precision=lax.Precision.HIGHEST
            )
        upper = from_root(block[:LEAD], "rows", 0)
        diag = jnp.linalg.cholesky(upper[low : low + PW])
        top_panel = lax.linalg.triangular_solve(
            diag, upper, left_side=False, lower=True, transpose_a=True
        )
        own_panel = lax.linalg.triangular_solve(
            diag, block, left_side=False, lower=True, transpose_a=True
        )
        top_panel = mask_panel(top_panel, top_ids, low)
        own_panel = mask_panel(own_panel, own_ids, low)
        if lead_rows is None:
            lead_rows, lead_top = (own_panel, top_panel)
        else:
            lead_rows = jnp.concatenate([lead_rows, own_panel], axis=1)
            lead_top = jnp.concatenate([lead_top, top_panel], axis=1)
    lead_rows = from_root(lead_rows, "cols", 0)
    copies = []
    for step in range(ratio):
        copies.append(from_root(lead_rows, "rows", col_pos * ratio + step))
    lead_cols = jnp.concatenate(copies, axis=0)
    return finish(
        row_points,
        row_noise,
        basis,
        row_starts,
        lead_rows,
        col_points,
        col_basis,
        col_start,
        lead_cols,
    )


def solution(mesh):
    placed = (P(), P(), P("rows", None))
    return jax.shard_map(
        body, mesh=mesh, in_specs=placed, out_specs=P("rows", "cols"), check_vma=False
    )
```

profile of v0, /device:TPU:1, one launch (start us, length us, event | category | flops | bytes accessed | tf_op | source)
XLA Modules:
  0.0 820.7 jit_solution(1879432131793466496)
XLA Ops:
  9.7 87.7 %all-reduce.13.cloned.1.call-done = f32[1280,128]{1,0:T(8,128)} async-done(((f32[1280,128]{1,0:T(8,128)}), f32[1280,128]{1,0:T(8,128)}) %all-reduce.13.cloned.1.call-update) | async-done | bytes 655376 | tf_op jit(solution)/shard_map/psum | solution.py:13
  98.3 40.4 %while.29 = (s32[]{:T(128)}, f32[10,128,512]{2,1,0:T(8,128)}, f32[10,127]{1,0:T(8,128)S(1)}, f32[4,127]{1,0:T(4,128)S(1)}, f32[10,128,128]{2,1,0:T(8,128)}, /*in...) while((s32[]{:T(128)}, f32[10,128,512]{2,1,0:T(8,128)}, ...), condition=%wide.region_3.4_spmd, body=%wide.region_1.0_spmd.sunk | while | flops 101157744 | bytes 1808469 | solution.py:46
  143.8 82.4 %all-reduce.15.cloned.1.call-done = f32[512,256]{0,1:T(8,128)} async-done(((f32[512,256]{0,1:T(8,128)}), f32[512,256]{0,1:T(8,128)}) %all-reduce.15.cloned.1.call-update) | async-done | bytes 524304 | tf_op jit(solution)/shard_map/psum | solution.py:13
  228.4 11.7 %cholesky.130 = f32[128,128]{1,0:T(8,128)S(1)} custom-call(f32[128,128]{1,0:T(8,128)S(1)} %cholesky.194), custom_call_target="Cholesky" | custom-call | tf_op jit(solution)/shard_map/jit(cholesky)/cholesky | solution.py:136
  240.2 9.8 %custom-call.17 = f32[1,128,128]{1,2,0:T(8,128)S(1)} custom-call(f32[1,128,128]{2,1,0:T(8,128)S(1)} %get-tuple-element.375), custom_call_target="InvertDiagBlocksLowerTriangular" | custom-call | tf_op jit(solution)/shard_map/jit(cholesky)/cholesky | solution.py:136
  250.5 11.7 %cholesky.147 = f32[128,128]{1,0:T(8,128)S(1)} custom-call(f32[128,128]{1,0:T(8,128)S(1)} %convolution_subtract_fusion.6), custom_call_target="Cholesky" | custom-call | tf_op jit(solution)/shard_map/jit(cholesky)/cholesky | solution.py:136
  265.0 5.4 while.31
  270.4 21.1 %custom-call.18 = f32[2,128,128]{1,2,0:T(8,128)} custom-call(f32[2,128,128]{2,1,0:T(8,128)} %get-tuple-element.280), custom_call_target="InvertDiagBlocksLowerTriangular" | custom-call | tf_op jit(solution)/shard_map/triangular_solve/custom-call.0 | solution.py:140
  300.3 85.1 %all-reduce.17.cloned.1.call-done = f32[512,256]{0,1:T(8,128)} async-done(((f32[512,256]{0,1:T(8,128)}), f32[512,256]{0,1:T(8,128)}) %all-reduce.17.cloned.1.call-update) | async-done | bytes 524304 | tf_op jit(solution)/shard_map/psum | solution.py:13
  387.5 11.7 %cholesky.164 = f32[128,128]{1,0:T(8,128)S(1)} custom-call(f32[128,128]{1,0:T(8,128)S(1)} %cholesky.197), custom_call_target="Cholesky" | custom-call | tf_op jit(solution)/shard_map/jit(cholesky)/cholesky | solution.py:136
  399.3 9.8 %custom-call.19 = f32[1,128,128]{1,2,0:T(8,128)S(1)} custom-call(f32[1,128,128]{2,1,0:T(8,128)S(1)} %get-tuple-element.371), custom_call_target="InvertDiagBlocksLowerTriangular" | custom-call | tf_op jit(solution)/shard_map/jit(cholesky)/cholesky | solution.py:136
  409.5 11.7 %cholesky.181 = f32[128,128]{1,0:T(8,128)S(1)} custom-call(f32[128,128]{1,0:T(8,128)S(1)} %convolution_subtract_fusion.5), custom_call_target="Cholesky" | custom-call | tf_op jit(solution)/shard_map/jit(cholesky)/cholesky | solution.py:136
  424.0 4.2 while.32
  428.2 19.7 %custom-call.20 = f32[2,128,128]{1,2,0:T(8,128)S(1)} custom-call(f32[2,128,128]{2,1,0:T(8,128)S(1)} %get-tuple-element.281), custom_call_target="InvertDiagBlocksLowerTriangular" | custom-call | tf_op jit(solution)/shard_map/triangular_solve/custom-call.0 | solution.py:140
  452.0 67.0 %all-reduce.19.cloned.1.call-done = f32[1280,512]{0,1:T(8,128)} async-done(((f32[1280,512]{0,1:T(8,128)}), f32[1280,512]{0,1:T(8,128)}) %all-reduce.19.cloned.1.call-update) | async-done | bytes 2621456 | tf_op jit(solution)/shard_map/psum | solution.py:13
  519.0 4.4 broadcast_select_fusion.1
  527.2 116.5 %all-reduce.21.cloned.1.call-done = (f32[1280,512]{0,1:T(8,128)}, f32[1280,512]{0,1:T(8,128)}, f32[1280,128]{1,0:T(8,128)}) async-done(((f32[1280,512]{0,1:T(8,128)}, f32[1280,512]{0,1:T(8,128)}, f32[1280,128]{1,0:T(8,128)}), (f32[1280,512]{0,1:T(8,128)}, f32[1280,512]{0,1:T(8,128)}, f32[1280,128]{1,0:T(8,128)})) %all-reduce.21.cloned.1.call-update) | async-done | bytes 5898256 | tf_op jit(solution)/shard_map/psum | solution.py:13
  643.8 5.5 maximum_bitcast_fusion
  650.5 162.4 %while.30 = (s32[]{:T(128)}, f32[10,128,2560]{2,1,0:T(8,128)}, f32[10,128,512]{2,1,0:T(8,128)}, s32[10]{0:T(128)S(1)}, f32[512,2560]{1,0:T(8,128)}, /*index=5*/f...) while((s32[]{:T(128)}, f32[10,128,2560]{2,1,0:T(8,128)}, ...), condition=%wide.region_16.19_spmd.clone.clone, body=%wide.region_14.18_spmd.clone.clone.sunk | while | flops 2519910400 | bytes 23683260 | solution.py:82
  659.8 6.9 fusion.100
  670.5 3.2 fusion.99
  676.1 6.9 fusion.100
  692.3 6.9 fusion.100
  703.1 3.2 fusion.99
  708.6 6.9 fusion.100
  724.8 6.9 fusion.100
  735.5 3.2 fusion.99
  741.1 6.9 fusion.100
  757.3 6.9 fusion.100
  773.5 6.9 fusion.100
  789.7 6.9 fusion.100
  806.0 6.9 fusion.100
  (458 shorter events, 161.0 us)
Async XLA Ops:
  6.5 2.4 copy-start
  6.5 90.8 %all-reduce.13.cloned.1.call-start = ((), (), s32[]{:S(2)}) async-start(), calls=%async_computation | async-start | bytes 1310720 | tf_op jit(solution)/shard_map/psum | solution.py:13
  8.8 217.3 %all-reduce.15.cloned.1.call-start = ((), (), s32[]{:S(2)}) async-start(), calls=%async_computation.1 | async-start | bytes 1048576 | tf_op jit(solution)/shard_map/psum | solution.py:13
  140.8 244.5 %all-reduce.17.cloned.1.call-start = ((), (), s32[]{:S(2)}) async-start(), calls=%async_computation.2 | async-start | bytes 1048576 | tf_op jit(solution)/shard_map/psum | solution.py:13
  227.3 64.3 %copy-start.4 = (f32[10,128,512]{2,1,0:T(8,128)S(1)}, f32[10,128,512]{2,1,0:T(8,128)}, u32[]{:S(2)}) copy-start(f32[10,128,512]{2,1,0:T(8,128)} %get-tuple-element.203) | copy-start | bytes 7864324
  262.3 2.0 copy-start.7
  264.2 29.0 %copy-start.5 = (f32[512,256]{0,1:T(8,128)S(1)}, f32[512,256]{0,1:T(8,128)}, u32[]{:S(2)}) copy-start(f32[512,256]{0,1:T(8,128)} %all-reduce.15.cloned.1.call-done) | copy-start | bytes 1572868
  291.5 1.7 copy-start.9
  296.4 1.3 copy-start.3
  300.0 219.0 %all-reduce.19.cloned.1.call-start = ((), (), s32[]{:S(2)}) async-start(), calls=%async_computation.3 | async-start | bytes 5242880 | tf_op jit(solution)/shard_map/psum | solution.py:13
  452.0 191.8 %all-reduce.21.cloned.1.call-start = ((), (), s32[]{:S(2)}) async-start(), calls=%async_computation.4 | async-start | bytes 11796480 | tf_op jit(solution)/shard_map/psum | solution.py:13
  523.4 1.7 copy-start.2
  643.8 5.5 copy-start.6
  643.8 5.5 copy-start.8
  812.9 0.9 copy-start.1
Sparse Core Ops, SparseCore 0:
  10.6 86.7 all-reduce.12
  141.0 85.1 all-reduce.14
  300.1 85.1 all-reduce.16
  452.1 66.8 all-reduce.18
  523.5 120.1 all-reduce.20
where the time goes:
time: 831 us; the launch traced here: 821 us
  waiting for transfers between devices  439 us (53%)
  other arithmetic  152 us (18%)
  matrix products  130 us (16%)
  local copies, waits for them, and re-layouts  74.6 us (9%)
  between operations  16.5 us (2%)
  loops' own time  8.69 us (1%)
    psum x5, waiting for transfers between devices, from_root(): return lax.psum(jnp.where(mine, x, jnp.zeros_like(x)), axis)  439 us
    dot_general x10, matrix products, finish_single(): trail = values - jnp.dot(lrow, cross, precision=lax.Precision.HIGHEST)  69.2 us
    another operation x13, other arithmetic, body(): diag = jnp.linalg.cholesky(upper[low:low + PW])  68.7 us
    dot_general x20, matrix products, point_rows(): jnp.dot(basis_row, col_basis.T, precision=lax.Precision.HIGHEST)  51.1 us
    another operation x5, other arithmetic, body(): lax.linalg.triangular_solve(diag, block, left_side=False, lower=True, tra...  40.8 us
  transfers between devices with their start and end apart: 5, of which 5 were waited for; matrix products, arithmetic and copies ran while one was open for 1% of the time, Pallas kernels for 0%

commit v1 on v0

v1 whole, which is shorter than its diff:
```python
import functools

import jax
import jax.numpy as jnp
from jax import lax
from jax.experimental import pallas as pl
from jax.experimental.pallas import tpu as pltpu
from jax.sharding import PartitionSpec as P

W = 128
LEAD = 512
CHUNK = 256
HIGHEST = lax.Precision.HIGHEST
MESH = pl.DeviceIdType.MESH
F32 = jnp.float32
BF16 = jnp.bfloat16


def dot(a, b, dims=((1,), (0,))):
    return lax.dot_general(a, b, (dims, ((), ())), precision=HIGHEST, preferred_element_type=F32)


def eye_mask():
    return lax.broadcasted_iota(jnp.int32, (W, W), 0) == lax.broadcasted_iota(jnp.int32, (W, W), 1)


def row_terms(xr, xj, noise, same):
    lane = lax.broadcasted_iota(jnp.int32, xr.shape, 1)
    rho = xr - xj
    k = jnp.exp(-0.5 * jnp.sum(rho * rho, axis=1, keepdims=True))
    kq = k * jnp.where(lane == 0, 1.0, rho)
    diagonal = jnp.where(lane == 0, 0.0, jnp.broadcast_to(k, xr.shape))
    return kq, diagonal + jnp.where(same, noise, 0.0)


def tile(eye, p, kq, diagonal):
    return jnp.where(eye, diagonal, 0.0) + p * kq


def exchange_kernel(n, basis, top, cols, scatter_send, scatter_recv, own_sem, top_send, top_recv, col_send, col_recv):
    me = lax.axis_index("rows")
    col = lax.axis_index("cols")
    rows = basis.shape[0]
    tp = LEAD // n
    cp = rows // n

    barrier = pltpu.get_barrier_semaphore()
    for k in range(1, n):
        pl.semaphore_signal(barrier, inc=1, device_id={"rows": lax.rem(me + k, n)}, device_id_type=MESH)
    pl.semaphore_wait(barrier, n - 1)

    def top_piece(ref, d):
        return ref.at[pl.ds(pl.multiple_of(d * tp, tp), tp), :]

    def src_piece(d):
        return basis.at[pl.ds(pl.multiple_of(d * cp, cp), cp), :]

    def col_piece(t, d):
        return cols.at[pl.ds(pl.multiple_of(t * rows + d * cp, cp), cp), :]

    def remote(src, dst, ss, rs, dest):
        return pltpu.make_async_remote_copy(
            src_ref=src, dst_ref=dst, send_sem=ss, recv_sem=rs, device_id={"rows": dest}, device_id_type=MESH
        )

    @pl.when(me == 0)
    def _():
        for k in range(1, n):
            d = lax.rem(me + k, n)
            remote(top_piece(basis, d), top_piece(top, d), scatter_send.at[0, k], scatter_recv.at[0], d).start()
        pltpu.make_async_copy(top_piece(basis, me), top_piece(top, me), own_sem.at[0]).start()

    for t in range(2):

        @pl.when(me == 2 * col + t)
        def _():
            for k in range(1, n):
                d = lax.rem(me + k, n)
                remote(src_piece(d), col_piece(t, d), scatter_send.at[1 + t, k], scatter_recv.at[1 + t], d).start()
            pltpu.make_async_copy(src_piece(me), col_piece(t, me), own_sem.at[1 + t]).start()

    @pl.when(me != 0)
    def _():
        remote(top_piece(top, me), top_piece(top, me), scatter_send.at[0, 0], scatter_recv.at[0], me).wait_recv()

    @pl.when(me == 0)
    def _():
        pltpu.make_async_copy(top_piece(basis, me), top_piece(top, me), own_sem.at[0]).wait()

    for k in range(1, n):
        d = lax.rem(me + k, n)
        remote(top_piece(top, me), top_piece(top, me), top_send.at[k], top_recv.at[k], d).start()

    for t in range(2):

        @pl.when(me != 2 * col + t)
        def _():
            remote(col_piece(t, me), col_piece(t, me), scatter_send.at[1 + t, 0], scatter_recv.at[1 + t], me).wait_recv()

        @pl.when(me == 2 * col + t)
        def _():
            pltpu.make_async_copy(src_piece(me), col_piece(t, me), own_sem.at[1 + t]).wait()

    for t in range(2):
        for k in range(1, n):
            d = lax.rem(me + k, n)
            remote(col_piece(t, me), col_piece(t, me), col_send.at[t, k], col_recv.at[t, k], d).start()

    for k in range(1, n):
        s = lax.rem(me + n - k, n)
        remote(top_piece(top, s), top_piece(top, s), top_send.at[k], top_recv.at[k], s).wait_recv()
    for t in range(2):
        for k in range(1, n):
            s = lax.rem(me + n - k, n)
            remote(col_piece(t, s), col_piece(t, s), col_send.at[t, k], col_recv.at[t, k], s).wait_recv()
    for k in range(1, n):
        remote(top_piece(top, me), top_piece(top, me), top_send.at[k], top_recv.at[k], me).wait_send()
    for t in range(2):
        for k in range(1, n):
            remote(col_piece(t, me), col_piece(t, me), col_send.at[t, k], col_recv.at[t, k], me).wait_send()

    @pl.when(me == 0)
    def _():
        for k in range(1, n):
            d = lax.rem(me + k, n)
            remote(top_piece(basis, d), top_piece(top, d), scatter_send.at[0, k], scatter_recv.at[0], d).wait_send()

    for t in range(2):

        @pl.when(me == 2 * col + t)
        def _():
            for k in range(1, n):
                d = lax.rem(me + k, n)
                remote(src_piece(d), col_piece(t, d), scatter_send.at[1 + t, k], scatter_recv.at[1 + t], d).wait_send()


def exchange(basis, n):
    vmem = pl.BlockSpec(memory_space=pltpu.VMEM)
    dma = pltpu.SemaphoreType.DMA
    return pl.pallas_call(
        functools.partial(exchange_kernel, n),
        out_shape=(
            jax.ShapeDtypeStruct((LEAD, W), F32),
            jax.ShapeDtypeStruct((2 * basis.shape[0], W), F32),
        ),
        in_specs=[vmem],
        out_specs=(vmem, vmem),
        scratch_shapes=[dma((3, n)), dma((3,)), dma((3,)), dma((n,)), dma((n,)), dma((2, n)), dma((2, n))],
        compiler_params=pltpu.CompilerParams(collective_id=0, has_side_effects=True),
        name="exchange",
    )(basis)


def factor_block(d):
    nb = W // 8
    a = [d[8 * i : 8 * i + 8, :] for i in range(nb)]
    lane = lax.broadcasted_iota(jnp.int32, (8, W), 1)
    sub = lax.broadcasted_iota(jnp.int32, (8, W), 0)
    e = [jnp.where(lane == sub + 8 * i, 1.0, 0.0).astype(F32) for i in range(nb)]
    scales = []
    for k in range(W):
        b, o = divmod(k, 8)
        col = [jnp.broadcast_to(a[i][:, k : k + 1], (8, W)) for i in range(b, nb)]
        pivot = jnp.broadcast_to(col[0][o : o + 1, :], (8, W))
        inv = 1.0 / pivot
        scales.append(lax.rsqrt(pivot[0:1, :]))
        arow = jnp.broadcast_to(a[b][o : o + 1, :], (8, W)) * inv
        erow = jnp.broadcast_to(e[b][o : o + 1, :], (8, W)) * inv
        for i in range(b, nb):
            c = col[i - b]
            if i == b:
                c = jnp.where(sub > o, c, 0.0)
            a[i] = a[i] - c * arow
            e[i] = e[i] - c * erow
    scale = [jnp.concatenate(scales[8 * i : 8 * i + 8], axis=0) for i in range(nb)]
    return jnp.concatenate([e[i] * scale[i] for i in range(nb)], axis=0)


def factor_kernel(top, xlead, xb, noise, out, s):
    eye = eye_mask()
    first = lax.broadcasted_iota(jnp.int32, (W, W), 0) == 0
    nlead = LEAD // W
    s[:, :LEAD] = dot(top[...], top[...], ((1,), (1,)))
    point = lax.broadcasted_iota(jnp.int32, (8, 1), 0)
    for j in range(nlead):
        kq, diagonal = row_terms(xlead[...], xlead[j : j + 1, :], noise[...], point == j)
        pj = jnp.where(first, 1.0, xb[j * W : (j + 1) * W, :])
        for i in range(nlead):
            p = pj - xb[i * W : (i + 1) * W, :]
            s[i * W : (i + 1) * W, j * W : (j + 1) * W] += tile(eye, p, kq[i : i + 1, :], diagonal[i : i + 1, :])
    ids = lax.broadcasted_iota(jnp.int32, (LEAD, LEAD), 0) == lax.broadcasted_iota(jnp.int32, (LEAD, LEAD), 1)
    s[:, LEAD:] = jnp.where(ids, 1.0, 0.0).astype(F32)
    lanes = lax.broadcasted_iota(jnp.int32, (W, LEAD), 1)

    def step(kb, _):
        at = pl.multiple_of(kb * W, W)
        inverse = factor_block(s[pl.ds(at, W), pl.ds(at, W)])
        panel = dot(inverse, s[pl.ds(at, W), :])
        coef = jnp.where(lanes >= (kb + 1) * W, panel[:, :LEAD], 0.0)
        s[...] -= dot(coef, panel, ((0,), (0,)))
        s[pl.ds(at, W), :] = panel
        return 0

    lax.fori_loop(0, nlead, step, 0)
    out[...] = s[:, LEAD:]


def factor(top, xlead, xb, noise):
    vmem = pl.BlockSpec(memory_space=pltpu.VMEM)
    return pl.pallas_call(
        factor_kernel,
        out_shape=jax.ShapeDtypeStruct((LEAD, LEAD), F32),
        in_specs=[vmem] * 4,
        out_specs=vmem,
        scratch_shapes=[pltpu.VMEM((LEAD, 2 * LEAD), F32)],
        compiler_params=pltpu.CompilerParams(vmem_limit_bytes=32 << 20),
        name="factor",
    )(top, xlead, xb, noise)


def split(v):
    hi = v.astype(BF16)
    return hi, (v - hi.astype(F32)).astype(BF16)


def main_kernel(row_pts, basis, top, inv, colb, xrow, xcol, xlead, xbrow, xbcol, xblead, noise_row, noise_lead, out, lead, lhs, rhs):
    row_pos = lax.axis_index("rows")
    col_pos = lax.axis_index("cols")
    step = pl.program_id(0)
    eye = eye_mask()
    first = lax.broadcasted_iota(jnp.int32, (W, W), 0) == 0
    nlead = LEAD // W
    half = LEAD // 2
    width = W + LEAD
    rpoint = row_pos * row_pts + lax.broadcasted_iota(jnp.int32, (xrow.shape[0], 1), 0)
    lpoint = lax.broadcasted_iota(jnp.int32, (xlead.shape[0], 1), 0)

    @pl.when(step == 0)
    def _():
        lead[...] = dot(basis[...], top[...], ((1,), (1,)))
        for j in range(nlead):
            kq, diagonal = row_terms(xrow[...], xlead[j : j + 1, :], noise_row[...], rpoint == j)
            pj = jnp.where(first, 1.0, xblead[j * W : (j + 1) * W, :])
            for i in range(row_pts):
                p = pj - xbrow[i * W : (i + 1) * W, :]
                lead[i * W : (i + 1) * W, j * W : (j + 1) * W] += tile(eye, p, kq[i : i + 1, :], diagonal[i : i + 1, :])

        def rows(i, _):
            at = pl.ds(pl.multiple_of(i * CHUNK, CHUNK), CHUNK)
            a = lead[at, :]
            left = dot(a[:, :half], inv[:half, :half], ((1,), (1,)))
            right = dot(a, inv[half:, :], ((1,), (1,)))
            lead[at, :half] = left
            lead[at, half:] = right
            for v, o in ((basis[at, :], 0), (left, W), (right, W + half)):
                hi, lo = split(v)
                n = v.shape[1]
                lhs[at, o : o + n] = hi
                lhs[at, width + o : width + o + n] = lo
                lhs[at, 2 * width + o : 2 * width + o + n] = hi
            return 0

        lax.fori_loop(0, basis.shape[0] // CHUNK, rows, 0)

    is_lead = jnp.logical_and(col_pos == 0, step < LEAD // CHUNK)

    @pl.when(is_lead)
    def _():
        cols = lax.broadcasted_iota(jnp.int32, (CHUNK, CHUNK), 1) + step * CHUNK
        at = pl.ds(pl.multiple_of(step * CHUNK, CHUNK), CHUNK)
        for i in range(basis.shape[0] // CHUNK):
            ids = lax.broadcasted_iota(jnp.int32, (CHUNK, CHUNK), 0) + i * CHUNK + row_pos * basis.shape[0]
            out[i * CHUNK : (i + 1) * CHUNK, :] = jnp.where(ids < cols, 0.0, lead[i * CHUNK : (i + 1) * CHUNK, at])

    @pl.when(jnp.logical_not(is_lead))
    def _():
        cb = colb[...]
        across = dot(top[...], cb, ((1,), (1,)))
        per = CHUNK // W
        base = step * per
        points = [xcol[pl.ds(base + t, 1), :] for t in range(per)]
        pjs = [jnp.where(first, 1.0, xbcol[t * W : (t + 1) * W, :]) for t in range(per)]
        ids = [col_pos * (row_pts * 2) + base + t for t in range(per)]
        terms = [row_terms(xlead[...], points[t], noise_lead[...], lpoint == ids[t]) for t in range(per)]
        pieces = []
        for i in range(nlead):
            strip = []
            for t in range(per):
                p = pjs[t] - xblead[i * W : (i + 1) * W, :]
                strip.append(tile(eye, p, terms[t][0][i : i + 1, :], terms[t][1][i : i + 1, :]))
            pieces.append(jnp.concatenate(strip, axis=1))
        across = across + jnp.concatenate(pieces, axis=0)
        upper = dot(inv[:half, :half], across[:half, :])
        lower = dot(inv[half:, :], across)
        hi, lo = split(cb.T)
        rhs[0:W, :] = hi
        rhs[width : width + W, :] = hi
        rhs[2 * width : 2 * width + W, :] = lo
        for v, o in ((upper, W), (lower, W + half)):
            hi, lo = split(-v)
            rhs[o : o + half, :] = hi
            rhs[width + o : width + o + half, :] = hi
            rhs[2 * width + o : 2 * width + o + half, :] = lo
        terms = [row_terms(xrow[...], points[t], noise_row[...], rpoint == ids[t]) for t in range(per)]
        two = CHUNK // W
        for i in range(row_pts // two):
            at = slice(i * CHUNK, (i + 1) * CHUNK)
            total = jnp.dot(lhs[at, :], rhs[...], preferred_element_type=F32)
            for u in range(two):
                q = i * two + u
                for t in range(per):
                    p = pjs[t] - xbrow[q * W : (q + 1) * W, :]
                    v = tile(eye, p, terms[t][0][q : q + 1, :], terms[t][1][q : q + 1, :])
                    out[q * W : (q + 1) * W, t * W : (t + 1) * W] = total[u * W : (u + 1) * W, t * W : (t + 1) * W] + v

        @pl.when(row_pos == 0)
        def _():
            out[:half, :] = upper
            out[half:LEAD, :] = lower


def main(row_pts, basis, top, inv, colb, xrow, xcol, xlead, xbrow, xbcol, xblead, noise_row, noise_lead):
    rows, cols = basis.shape[0], colb.shape[0]
    width = W + LEAD

    def whole(v):
        return pl.BlockSpec(v.shape, lambda j: (0, 0), pipeline_mode=pl.Buffered(1))

    chunk = pl.BlockSpec((CHUNK, W), lambda j: (j, 0))
    return pl.pallas_call(
        functools.partial(main_kernel, row_pts),
        out_shape=jax.ShapeDtypeStruct((rows, cols), F32),
        grid=(cols // CHUNK,),
        in_specs=[whole(basis), whole(top), whole(inv), chunk, whole(xrow), whole(xcol), whole(xlead), whole(xbrow), chunk, whole(xblead), whole(noise_row), whole(noise_lead)],
        out_specs=pl.BlockSpec((rows, CHUNK), lambda j: (0, j)),
        scratch_shapes=[
            pltpu.VMEM((rows, LEAD), F32),
            pltpu.VMEM((rows, 3 * width), BF16),
            pltpu.VMEM((3 * width, CHUNK), BF16),
        ],
        compiler_params=pltpu.CompilerParams(vmem_limit_bytes=48 << 20),
        name="output",
    )(basis, top, inv, colb, xrow, xcol, xlead, xbrow, xbcol, xblead, noise_row, noise_lead)


def pad_rows(v, n):
    return jnp.pad(v, ((0, n - v.shape[0]), (0, 0)))


def body(points, noise, basis):
    row_pos = lax.axis_index("rows")
    col_pos = lax.axis_index("cols")
    n = lax.axis_size("rows")
    row_pts = basis.shape[0] // W
    col_pts = 2 * row_pts
    nlead = LEAD // W
    x = jnp.pad(points, ((0, 0), (1, 0)))
    xrow = lax.dynamic_slice_in_dim(x, row_pos * row_pts, row_pts, 0)
    xcol = lax.dynamic_slice_in_dim(x, col_pos * col_pts, col_pts, 0)
    nrow = lax.dynamic_slice_in_dim(noise, row_pos * row_pts, row_pts, 0)

    def spread(v):
        return jnp.broadcast_to(v[:, :, None], v.shape + (W,)).reshape(-1, W)

    xlead = x[:nlead]
    xblead = spread(xlead)
    top, cols = exchange(basis, n)
    inv = factor(top, pad_rows(xlead, 8), xblead, pad_rows(noise[:nlead], 8))
    return main(
        row_pts, basis, top, inv, cols, pad_rows(xrow, 16), pad_rows(xcol, 24), pad_rows(xlead, 8),
        spread(xrow), spread(xcol), xblead, pad_rows(nrow, 16), pad_rows(noise[:nlead], 8),
    )


def solution(mesh):
    placed = (P(), P(), P("rows", None))
    return jax.shard_map(body, mesh=mesh, in_specs=placed, out_specs=P("rows", "cols"), check_vma=False)
```

time: 831 us -> 166 us (0.20)
  waiting for transfers between devices: 439 us -> 0 us
  Pallas kernels: 0 us -> 158 us
  other arithmetic: 152 us -> 0.79 us
  matrix products: 130 us -> 0 us
  local copies, waits for them, and re-layouts: 74.6 us -> 4.97 us
  between operations: 16.5 us -> 0.1 us
  loops' own time: 8.69 us -> 0 us
    psum x5 -> x0, waiting for transfers between devices: 439 us -> none  [from_root(): return lax.psum(jnp.where(mine, x, jnp.zeros_like(x)), axis)]
    pallas_call x0 -> x3, Pallas kernels: none -> 158 us  [the longest x1 78.7 us: factor(): pl.pallas_call(factor_kernel, out_shape=jax.ShapeDtypeStruct((LEAD, LEAD)...]
    dot_general x31 -> x0, matrix products: 122 us -> none  [the longest x10 69.2 us: finish_single(): trail = values - jnp.dot(lrow, cross, precision=lax.Precision.HIGHEST)]
    another operation x18 -> x0, other arithmetic: 109 us -> none  [the longest x13 68.7 us: body(): diag = jnp.linalg.cholesky(upper[low:low + PW])]
    add x30 -> x0, local copies, waits for them, and re-layouts: 16.3 us -> none  [tile_rows(): jmat[:, None, :] + left.T[:, :, None] * right[None, :, :]]
    add x43 -> x0, other arithmetic: 13.2 us -> none  [the longest x10 6.71 us: finish_single(): row_ids = start + jnp.arange(width)]
    dynamic_slice x23 -> x2, local copies, waits for them, and re-layouts: 13.8 us -> 1.59 us  [the longest x1 0.8 us: body(): xrow = lax.dynamic_slice_in_dim(x, row_pos * row_pts, row_pts, 0)]
    select_n x27 -> x0, other arithmetic: 11.2 us -> none  [the longest x5 10 us: from_root(): return lax.psum(jnp.where(mine, x, jnp.zeros_like(x)), axis)]
  transfers between devices with their start and end apart: 5 -> 0, of which waited for: 5 -> 0; matrix products, arithmetic and copies ran while one was open for 1% -> 0% of each run, Pallas kernels for 0% -> 0%
where the time goes in v1:
time: 166 us; the launch traced here: 164 us
  Pallas kernels  158 us (95%)
  local copies, waits for them, and re-layouts  4.97 us (3%)
    pallas_call x1, Pallas kernels, factor(): pl.pallas_call(factor_kernel, out_shape=jax.ShapeDtypeStruct((LEAD, LEAD)...  78.7 us
    pallas_call x1, Pallas kernels, main(): pl.pallas_call(functools.partial(main_kernel, row_pts), out_shape=jax.Sha...  47.1 us
    pallas_call x1, Pallas kernels, exchange(): pl.pallas_call(functools.partial(exchange_kernel, n), out_shape=(jax.Shap...  32.1 us

profile of v1, /device:TPU:1, one launch (start us, length us, event | category | flops | bytes accessed | tf_op | source)
XLA Modules:
  0.0 163.7 jit_solution(16088143175650935998)
XLA Ops:
  0.0 0.8 fusion.1
  0.8 0.8 slice_select_fusion
  1.6 0.8 fusion.2
  2.3 0.8 pad_dynamic-slice_fusion
  3.1 0.8 pad_dynamic-slice_fusion.1
  4.0 0.1 broadcast_in_dim.25.xb.xblead
  4.1 0.2 broadcast_in_dim.27.xbrow
  4.3 0.4 broadcast_in_dim.29.xbcol
  4.7 0.0 copy-start
  4.7 32.1 %exchange.1 = (f32[512,128]{1,0:T(8,128)}, f32[2560,128]{1,0:T(8,128)}) custom-call(f32[1280,128]{1,0:T(8,128)} %basis.3), custom_call_target="tpu_custom_call" | custom-call | tf_op jit(solution)/shard_map/exchange/pallas_call | solution.py:140
  36.8 0.0 copy-start.1
  36.9 0.0 copy-start.2
  36.9 1.0 copy-done.2
  37.9 0.0 copy-start.3
  37.9 78.7 %factor.1.inv = f32[512,512]{1,0:T(8,128)S(1)} custom-call(f32[512,128]{1,0:T(8,128)S(1)} %copy-done.2, f32[8,128]{1,0:T(8,128)S(1)} %get-tuple-element.10.xlead, f32[512,128]{1,0:T(8,128)S(1)} %broadcast_in_dim.25.xb.xblead, f32[8,128]{1,0:T(8,128)S(1)} %get-tuple-element.9.noise.noise_lead), custom_call_target="tpu_custom_call" | custom-call | tf_op jit(solution)/shard_map/factor/pallas_call | solution.py:210
  116.6 0.0 copy-done
  116.6 0.0 copy-done.1
  116.6 0.0 copy-done.3
  116.6 47.1 %output.1 = f32[1280,2560]{1,0:T(8,128)} custom-call(f32[1280,128]{1,0:T(8,128)S(1)} %copy-done, f32[512,128]{1,0:T(8,128)S(1)} %copy-done.3, f32[512,512]{1,0:T(8,128)S(1)} %factor.1.inv, f32[2560,128]{1,0:T(8,128)S(1)} %copy-done.1, f32[16,128]{1,0:T(8,128)S(1)} %pad.27.xrow, f32[24,128]{1,0:T(8,128)S(1)} %pad.28.xcol, ...), custom_call_target="tpu_custom_call" | custom-call | tf_op jit(solution)/shard_map/output/pallas_call | solution.py:330
  (3 shorter events, 0.0 us)
Async XLA Ops:
  4.7 111.9 %copy-start = (f32[1280,128]{1,0:T(8,128)S(1)}, f32[1280,128]{1,0:T(8,128)}, u32[]{:S(2)}) copy-start(f32[1280,128]{1,0:T(8,128)} %basis.3) | copy-start | bytes 1966084
  36.8 79.8 %copy-start.1 = (f32[2560,128]{1,0:T(8,128)S(1)}, f32[2560,128]{1,0:T(8,128)}, u32[]{:S(2)}) copy-start(f32[2560,128]{1,0:T(8,128)} %get-tuple-element.8.colb) | copy-start | bytes 3932164
  36.9 1.1 copy-start.2
  37.9 78.7 %copy-start.3 = (f32[512,128]{1,0:T(8,128)S(1)}, f32[512,128]{1,0:T(8,128)}, u32[]{:S(2)}) copy-start(f32[512,128]{1,0:T(8,128)} %get-tuple-element.7.top) | copy-start | bytes 786436
